TPU v7x, 256 devices: a whole 4x4x8 slice. The times are simulated.
256 devices in a mesh: segment: 8 (over y, z_lo), frame: 32 (over x, z_hi, core).
Axes of the slice: x: 4, y: 4, z: 8 (z_hi: 4, z_lo: 2; z = z_hi * 2 + z_lo), core: 2. Of those that a mesh axis runs over, the one named last changes fastest.
Arguments:
- noisy_clips: bfloat16 [4, 32, 16, 16, 512], P(None, 'frame'), may hold values from -6 to 6
- conv_first: bfloat16 [8, 9, 512, 512], P('segment', None, 'frame'), may hold values from -0.09375 to 0.09375
- conv_second: bfloat16 [8, 9, 512, 512], P('segment', None, 'frame'), may hold values from -0.09375 to 0.09375
- temporal: bfloat16 [8, 3, 512, 512], P('segment', None, 'frame'), may hold values from -0.15625 to 0.15625
Outputs:
- denoised: bfloat16 [4, 32, 16, 16, 512], P(None, 'frame', 'segment')
All inputs are finite; a program needn't handle non-finite values.
Results may differ from a plain program's by a relative error of at most 0.013.
Values may be sent and summed in bfloat16 or wider, within the bound.
No kernel may reach another device: no remote copies, remote signals or barrier semaphores. Data moves between devices by JAX's collectives and lax.ppermute only.
A program may use at most 64 MiB of HBM per device.

v0:
```python
import jax
import jax.numpy as jnp
from jax import lax
from jax.sharding import PartitionSpec as P

skip_scale = 0.7071067811865476


def passed_along(shard, axis, by):
    length = lax.axis_size(axis)
    pairs = [(i, i + by) for i in range(length) if 0 <= i + by < length]
    return lax.ppermute(shard, axis, pairs)


def partner(shard, axis, bit):
    return lax.ppermute(shard, axis, [(i, i ^ 1 << bit) for i in range(lax.axis_size(axis))])


def extended_2(cells, sides, width):
    for axis, dim in sides:
        count = lax.axis_size(axis)
        ends = count - 1
        head = lax.slice_in_dim(cells, 0, width, axis=dim)
        tail = lax.slice_in_dim(cells, cells.shape[dim] - width, cells.shape[dim], axis=dim)
        cells = jnp.concatenate(
            [
                lax.ppermute(tail, axis, [(i, (i + 1) % count) for i in range(ends)]),
                cells,
                lax.ppermute(head, axis, [((i + 1) % count, i) for i in range(ends)]),
            ],
            axis=dim,
        )
    return cells


def broadcast(shard, axis, root):
    mine = lax.axis_index(axis) == root
    return lax.psum(jnp.where(mine, shard, jnp.zeros_like(shard)), axis)


def spatial(field_in, kernel):
    extent = field_in.shape[1]
    channels = field_in.shape[3]
    padded = jnp.pad(field_in, ((0, 0), (1, 1), (1, 1), (0, 0)))
    accumulated = jnp.zeros((field_in.shape[0] * extent * extent, channels), jnp.float32)
    for row_shift in range(3):
        for col_shift in range(3):
            window = padded[
                :, row_shift : row_shift + extent, col_shift : col_shift + extent, :
            ].reshape(-1, channels)
            accumulated = accumulated + jnp.dot(
                window, kernel[3 * row_shift + col_shift], preferred_element_type=jnp.float32
            )
    return accumulated.reshape(field_in.shape)


def temporal_mix(extended, kernel, frame_local):
    channels = extended.shape[3]
    out_shape = (frame_local,) + extended.shape[1:]
    accumulated = jnp.zeros(out_shape, jnp.float32)
    for offset in range(3):
        window = extended[offset : offset + frame_local].reshape(-1, channels)
        accumulated = accumulated + jnp.dot(
            window, kernel[offset], preferred_element_type=jnp.float32
        ).reshape(out_shape)
    return accumulated


def on_device(noisy_clips, conv_first, conv_second, temporal):
    sections = lax.axis_size("segment")
    segment_id = lax.axis_index("segment")
    first_full, second_full, time_full = (
        lax.all_gather(conv_first, "frame", axis=2, tiled=True),
        lax.all_gather(conv_second, "frame", axis=2, tiled=True),
        lax.all_gather(temporal, "frame", axis=2, tiled=True),
    )
    first_kernel = first_full[0]
    second_kernel = second_full[0]
    time_kernel = time_full[0]
    clip_count = noisy_clips.shape[0]
    frame_local = noisy_clips.shape[1]
    side_len = noisy_clips.shape[2]
    block_shape = noisy_clips.shape[1:]
    tick_count = clip_count + sections - 1
    half_sections = sections // 2
    is_up = segment_id >= half_sections
    side_store = jnp.zeros((clip_count,) + block_shape, jnp.bfloat16)
    out_store = jnp.zeros(noisy_clips.shape, jnp.bfloat16)
    prev_out = jnp.zeros(block_shape, jnp.bfloat16)

    def tick_step(carry, tick_index):
        prev_out, side_store, out_store = carry
        clip_now = tick_index - segment_id
        active = (clip_now >= 0) & (clip_now < clip_count)
        clip_slot = jnp.clip(clip_now, 0, clip_count - 1)
        own_input = lax.dynamic_index_in_dim(noisy_clips, clip_slot, 0, keepdims=False)
        received = passed_along(prev_out, "segment", 1)
        entering = jnp.where(segment_id == 0, own_input, received)
        mirrored = entering
        for bit_number in range(sections.bit_length() - 1):
            mirrored = partner(mirrored, "segment", bit_number)
        mirror_clip = tick_index - (sections - 1 - segment_id)
        written = (jnp.arange(clip_count) == mirror_clip) & is_up
        side_store = jnp.where(written[:, None, None, None, None], mirrored[None], side_store)
        skip_feature = lax.dynamic_index_in_dim(side_store, clip_slot, 0, keepdims=False)
        joined = (
            (entering.astype(jnp.float32) + skip_feature.astype(jnp.float32)) * skip_scale
        ).astype(jnp.bfloat16)
        section_in = jnp.where(is_up, joined, entering)
        activated = lax.cond(
            active,
            lambda: jax.nn.silu(spatial(section_in, first_kernel)).astype(jnp.bfloat16),
            lambda: jnp.zeros(block_shape, jnp.bfloat16),
        )
        extended = extended_2(activated, (("frame", 0),), 1)

        def second_pass():
            branch_sum = spatial(activated, second_kernel) + temporal_mix(
                extended, time_kernel, frame_local
            )
            return (section_in.astype(jnp.float32) + jax.nn.silu(branch_sum)).astype(jnp.bfloat16)

        section_out = lax.cond(active, second_pass, lambda: jnp.zeros(block_shape, jnp.bfloat16))
        finished = (jnp.arange(clip_count) == clip_slot) & active & (segment_id == sections - 1)
        out_store = jnp.where(finished[:, None, None, None, None], section_out[None], out_store)
        return ((section_out, side_store, out_store), None)

    final_carry, unused = lax.scan(
        tick_step, (prev_out, side_store, out_store), jnp.arange(tick_count, dtype=jnp.int32)
    )
    delivered = broadcast(final_carry[2], "segment", sections - 1)
    slab_rows = side_len // sections
    return lax.dynamic_slice_in_dim(delivered, segment_id * slab_rows, slab_rows, 2)


def solution(mesh):
    in_specs = (
        P(None, "frame", None, None, None),
        P("segment", None, "frame", None),
        P("segment", None, "frame", None),
        P("segment", None, "frame", None),
    )
    out_specs = P(None, "frame", "segment", None, None)
    return jax.shard_map(
        on_device, mesh=mesh, in_specs=in_specs, out_specs=out_specs, check_vma=False
    )
```

profile of v0, /device:TPU:2, one launch (start us, length us, event | category | flops | bytes accessed | tf_op | source)
XLA Modules:
  0.0 975.8 jit_solution(13421447813197799213)
XLA Ops:
  8.8 56.3 %all-gather.8.cloned.1.call-done = bf16[1,3,512,512]{3,2,1,0:T(8,128)(2,1)} async-done(((bf16[1,3,16,512]{3,2,1,0:T(8,128)(2,1)}), bf16[1,3,512,512]{3,2,1,0:T(8,128)(2,1)}) %all-gather.8.cloned.1.call-update) | async-done | bytes 1572880 | tf_op jit(solution)/shard_map/all_gather | solution.py:75
  65.1 63.4 %all-gather.4.cloned.1.call-done = bf16[1,9,512,512]{3,2,1,0:T(8,128)(2,1)} async-done(((bf16[1,9,16,512]{3,2,1,0:T(8,128)(2,1)}), bf16[1,9,512,512]{3,2,1,0:T(8,128)(2,1)}) %all-gather.4.cloned.1.call-update) | async-done | bytes 4718608 | tf_op jit(solution)/shard_map/all_gather | solution.py:73
  128.4 63.1 %all-gather.6.cloned.1.call-done = bf16[1,9,512,512]{3,2,1,0:T(8,128)(2,1)} async-done(((bf16[1,9,16,512]{3,2,1,0:T(8,128)(2,1)}), bf16[1,9,512,512]{3,2,1,0:T(8,128)(2,1)}) %all-gather.6.cloned.1.call-update) | async-done | bytes 4718608 | tf_op jit(solution)/shard_map/all_gather | solution.py:74
  192.3 682.3 %while.16 = (s32[]{:T(128)}, bf16[1,16,16,512]{3,2,1,0:T(8,128)(2,1)}, bf16[4,1,16,16,512]{4,3,2,1,0:T(8,128)(2,1)S(1)}, bf16[4,1,16,16,512]{4,3,2,1,0:T(8,128)(...) while((s32[]{:T(128)}, ...), condition=%wide.region_5.6_spmd.clone, body=%wide.region_0.5_spmd.clone.sunk | while | flops 2825650176 | bytes 99615424 | solution.py:128
  234.9 6.7 collective-permute-start.5
  245.5 7.0 conditional.7
  270.5 7.6 collective-permute-done.2
  278.8 7.2 collective-permute-done.3
  293.9 6.7 collective-permute-start.5
  307.3 7.0 conditional.7
  342.1 7.3 collective-permute-done.3
  357.3 6.7 collective-permute-start.5
  370.6 7.0 conditional.7
  397.8 7.7 collective-permute-done.2
  406.1 7.2 collective-permute-done.3
  421.2 6.7 collective-permute-start.5
  434.5 7.0 conditional.7
  468.4 7.5 collective-permute-done.3
  478.5 6.7 collective-permute-start.5
  491.1 14.6 %collective-permute-start = (bf16[1,16,16,512]{3,2,1,0:T(8,128)(2,1)}, bf16[1,16,16,512]{3,2,1,0:T(8,128)(2,1)S(1)}, u32[]{:S(2)}, u32[]{:S(2)}) collective-permute-start(bf16[1,16,16,512]{3,2,1,0:T(8,128)(2,1)} %get-tuple-element.343), channel_id=1, source_target_pairs={{0,32},{32,64},{64,96},{96,128},{128,160},{160,192},{192,224},{1,3... | collective-permute-start | bytes 786440 | tf_op jit(solution)/shard_map/while/body/eval_jaxpr/ppermute | solution.py:12
  510.8 6.9 collective-permute-start.1
  531.0 7.2 collective-permute-done.3
  562.9 15.2 %collective-permute-start.1 = (bf16[1,16,16,512]{3,2,1,0:T(8,128)(2,1)S(1)}, bf16[1,16,16,512]{3,2,1,0:T(8,128)(2,1)S(1)}, u32[]{:S(2)}, u32[]{:S(2)}) collective-permute-start(bf16[1,16,16,512]{3,2,1,0:T(8,128)(2,1)S(1)} %bitcast_select_fusion.2), channel_id=1, source_target_pairs={{0,32},{32,0},{64,96},{96,64},{128,160},{160,128},{192,224},{224,1... | collective-permute-start | bytes 786440 | tf_op jit(solution)/shard_map/while/body/eval_jaxpr/ppermute | solution.py:16
  594.0 7.3 collective-permute-done.3
  603.8 6.7 collective-permute-start.5
  637.9 11.0 %collective-permute-start.2 = (bf16[1,16,16,512]{3,2,1,0:T(8,128)(2,1)S(1)}, bf16[1,16,16,512]{3,2,1,0:T(8,128)(2,1)S(1)}, u32[]{:S(2)}, u32[]{:S(2)}) collective-permute-start(bf16[1,16,16,512]{3,2,1,0:T(8,128)(2,1)S(1)} %collective-permute-done.1), channel_id=1, source_target_pairs={{0,64},{32,96},{64,0},{96,32},{128,192},{160,224},{192,128},{224,1... | collective-permute-start | bytes 786440 | tf_op jit(solution)/shard_map/while/body/eval_jaxpr/ppermute | solution.py:16
  666.8 6.7 collective-permute-start.5
  699.2 13.0 %collective-permute-start.2 = (bf16[1,16,16,512]{3,2,1,0:T(8,128)(2,1)S(1)}, bf16[1,16,16,512]{3,2,1,0:T(8,128)(2,1)S(1)}, u32[]{:S(2)}, u32[]{:S(2)}) collective-permute-start(bf16[1,16,16,512]{3,2,1,0:T(8,128)(2,1)S(1)} %collective-permute-done.1), channel_id=1, source_target_pairs={{0,64},{32,96},{64,0},{96,32},{128,192},{160,224},{192,128},{224,1... | collective-permute-start | bytes 786440 | tf_op jit(solution)/shard_map/while/body/eval_jaxpr/ppermute | solution.py:16
  767.6 19.2 %collective-permute-start.3 = (bf16[1,16,16,512]{3,2,1,0:T(8,128)(2,1)S(1)}, bf16[1,16,16,512]{3,2,1,0:T(8,128)(2,1)S(1)}, u32[]{:S(2)}, u32[]{:S(2)}) collective-permute-start(bf16[1,16,16,512]{3,2,1,0:T(8,128)(2,1)S(1)} %collective-permute-done.2), channel_id=1, source_target_pairs={{0,128},{32,160},{64,192},{96,224},{128,0},{160,32},{192,64},{224,... | collective-permute-start | bytes 786440 | tf_op jit(solution)/shard_map/while/body/eval_jaxpr/ppermute | solution.py:16
  793.6 6.7 collective-permute-start.5
  835.9 15.5 %collective-permute-start.3 = (bf16[1,16,16,512]{3,2,1,0:T(8,128)(2,1)S(1)}, bf16[1,16,16,512]{3,2,1,0:T(8,128)(2,1)S(1)}, u32[]{:S(2)}, u32[]{:S(2)}) collective-permute-start(bf16[1,16,16,512]{3,2,1,0:T(8,128)(2,1)S(1)} %collective-permute-done.2), channel_id=1, source_target_pairs={{0,128},{32,160},{64,192},{96,224},{128,0},{160,32},{192,64},{224,... | collective-permute-start | bytes 786440 | tf_op jit(solution)/shard_map/while/body/eval_jaxpr/ppermute | solution.py:16
  875.7 92.0 %all-reduce.4.cloned.1.call-done = bf16[4,1,16,16,512]{4,3,2,1,0:T(8,128)(2,1)} async-done(((bf16[4,1,16,16,512]{4,3,2,1,0:T(8,128)(2,1)}), bf16[4,1,16,16,512]{4,3,2,1,0:T(8,128)(2,1)}) %all-reduce.4.cloned.1.call-update) | async-done | bytes 1048592 | tf_op jit(solution)/shard_map/psum | solution.py:38
  (352 shorter events, 490.3 us)
Async XLA Ops:
  6.5 58.5 %all-gather.8.cloned.1.call-start = ((), (), s32[]{:S(2)}) async-start(), calls=%async_computation.2 | async-start | bytes 1622016 | tf_op jit(solution)/shard_map/all_gather | solution.py:75
  7.3 121.2 %all-gather.4.cloned.1.call-start = ((), (), s32[]{:S(2)}) async-start(), calls=%async_computation | async-start | bytes 4866048 | tf_op jit(solution)/shard_map/all_gather | solution.py:73
  8.0 183.6 %all-gather.6.cloned.1.call-start = ((), (), s32[]{:S(2)}) async-start(), calls=%async_computation.1 | async-start | bytes 4866048 | tf_op jit(solution)/shard_map/all_gather | solution.py:74
  8.7 959.0 %all-reduce.4.cloned.1.call-start = ((), (), s32[]{:S(2)}) async-start(), calls=%async_computation.3 | async-start | bytes 2097152 | tf_op jit(solution)/shard_map/psum | solution.py:38
  233.0 10.7 %collective-permute-start.4 = (bf16[1,16,16,512]{3,2,1,0:T(8,128)(2,1)S(1)}, bf16[1,16,16,512]{3,2,1,0:T(8,128)(2,1)S(1)}, u32[]{:S(2)}, u32[]{:S(2)}) collective-permute-start(bf16[1,16,16,512]{3,2,1,0:T(8,128)(2,1)S(1)} %get-tuple-element.378), channel_id=1, source_target_pairs={{0,1},{1,2},{2,3},{3,4},{4,5},{5,6},{6,7},{7,8},{8,9},{9,10},{10,1... | collective-permute-start | bytes 786440 | tf_op jit(solution)/shard_map/while/body/eval_jaxpr/ppermute | solution.py:27
  292.0 10.9 %collective-permute-start.4 = (bf16[1,16,16,512]{3,2,1,0:T(8,128)(2,1)S(1)}, bf16[1,16,16,512]{3,2,1,0:T(8,128)(2,1)S(1)}, u32[]{:S(2)}, u32[]{:S(2)}) collective-permute-start(bf16[1,16,16,512]{3,2,1,0:T(8,128)(2,1)S(1)} %get-tuple-element.378), channel_id=1, source_target_pairs={{0,1},{1,2},{2,3},{3,4},{4,5},{5,6},{6,7},{7,8},{8,9},{9,10},{10,1... | collective-permute-start | bytes 786440 | tf_op jit(solution)/shard_map/while/body/eval_jaxpr/ppermute | solution.py:27
  293.9 13.4 %collective-permute-start.5 = (bf16[1,16,16,512]{3,2,1,0:T(8,128)(2,1)S(1)}, bf16[1,16,16,512]{3,2,1,0:T(8,128)(2,1)S(1)}, u32[]{:S(2)}, u32[]{:S(2)}) collective-permute-start(bf16[1,16,16,512]{3,2,1,0:T(8,128)(2,1)S(1)} %get-tuple-element.378), channel_id=1, source_target_pairs={{1,0},{2,1},{3,2},{4,3},{5,4},{6,5},{7,6},{8,7},{9,8},{10,9},{11,1... | collective-permute-start | bytes 786440 | tf_op jit(solution)/shard_map/while/body/eval_jaxpr/ppermute | solution.py:29
  355.3 10.8 %collective-permute-start.4 = (bf16[1,16,16,512]{3,2,1,0:T(8,128)(2,1)S(1)}, bf16[1,16,16,512]{3,2,1,0:T(8,128)(2,1)S(1)}, u32[]{:S(2)}, u32[]{:S(2)}) collective-permute-start(bf16[1,16,16,512]{3,2,1,0:T(8,128)(2,1)S(1)} %get-tuple-element.378), channel_id=1, source_target_pairs={{0,1},{1,2},{2,3},{3,4},{4,5},{5,6},{6,7},{7,8},{8,9},{9,10},{10,1... | collective-permute-start | bytes 786440 | tf_op jit(solution)/shard_map/while/body/eval_jaxpr/ppermute | solution.py:27
  357.3 13.4 %collective-permute-start.5 = (bf16[1,16,16,512]{3,2,1,0:T(8,128)(2,1)S(1)}, bf16[1,16,16,512]{3,2,1,0:T(8,128)(2,1)S(1)}, u32[]{:S(2)}, u32[]{:S(2)}) collective-permute-start(bf16[1,16,16,512]{3,2,1,0:T(8,128)(2,1)S(1)} %get-tuple-element.378), channel_id=1, source_target_pairs={{1,0},{2,1},{3,2},{4,3},{5,4},{6,5},{7,6},{8,7},{9,8},{10,9},{11,1... | collective-permute-start | bytes 786440 | tf_op jit(solution)/shard_map/while/body/eval_jaxpr/ppermute | solution.py:29
  419.2 10.8 %collective-permute-start.4 = (bf16[1,16,16,512]{3,2,1,0:T(8,128)(2,1)S(1)}, bf16[1,16,16,512]{3,2,1,0:T(8,128)(2,1)S(1)}, u32[]{:S(2)}, u32[]{:S(2)}) collective-permute-start(bf16[1,16,16,512]{3,2,1,0:T(8,128)(2,1)S(1)} %get-tuple-element.378), channel_id=1, source_target_pairs={{0,1},{1,2},{2,3},{3,4},{4,5},{5,6},{6,7},{7,8},{8,9},{9,10},{10,1... | collective-permute-start | bytes 786440 | tf_op jit(solution)/shard_map/while/body/eval_jaxpr/ppermute | solution.py:27
  421.2 13.3 %collective-permute-start.5 = (bf16[1,16,16,512]{3,2,1,0:T(8,128)(2,1)S(1)}, bf16[1,16,16,512]{3,2,1,0:T(8,128)(2,1)S(1)}, u32[]{:S(2)}, u32[]{:S(2)}) collective-permute-start(bf16[1,16,16,512]{3,2,1,0:T(8,128)(2,1)S(1)} %get-tuple-element.378), channel_id=1, source_target_pairs={{1,0},{2,1},{3,2},{4,3},{5,4},{6,5},{7,6},{8,7},{9,8},{10,9},{11,1... | collective-permute-start | bytes 786440 | tf_op jit(solution)/shard_map/while/body/eval_jaxpr/ppermute | solution.py:29
  476.5 10.7 %collective-permute-start.4 = (bf16[1,16,16,512]{3,2,1,0:T(8,128)(2,1)S(1)}, bf16[1,16,16,512]{3,2,1,0:T(8,128)(2,1)S(1)}, u32[]{:S(2)}, u32[]{:S(2)}) collective-permute-start(bf16[1,16,16,512]{3,2,1,0:T(8,128)(2,1)S(1)} %get-tuple-element.378), channel_id=1, source_target_pairs={{0,1},{1,2},{2,3},{3,4},{4,5},{5,6},{6,7},{7,8},{8,9},{9,10},{10,1... | collective-permute-start | bytes 786440 | tf_op jit(solution)/shard_map/while/body/eval_jaxpr/ppermute | solution.py:27
  491.1 18.7 %collective-permute-start = (bf16[1,16,16,512]{3,2,1,0:T(8,128)(2,1)}, bf16[1,16,16,512]{3,2,1,0:T(8,128)(2,1)S(1)}, u32[]{:S(2)}, u32[]{:S(2)}) collective-permute-start(bf16[1,16,16,512]{3,2,1,0:T(8,128)(2,1)} %get-tuple-element.343), channel_id=1, source_target_pairs={{0,32},{32,64},{64,96},{96,128},{128,160},{160,192},{192,224},{1,3... | collective-permute-start | bytes 786440 | tf_op jit(solution)/shard_map/while/body/eval_jaxpr/ppermute | solution.py:12
  510.8 11.3 %collective-permute-start.1 = (bf16[1,16,16,512]{3,2,1,0:T(8,128)(2,1)S(1)}, bf16[1,16,16,512]{3,2,1,0:T(8,128)(2,1)S(1)}, u32[]{:S(2)}, u32[]{:S(2)}) collective-permute-start(bf16[1,16,16,512]{3,2,1,0:T(8,128)(2,1)S(1)} %bitcast_select_fusion.2), channel_id=1, source_target_pairs={{0,32},{32,0},{64,96},{96,64},{128,160},{160,128},{192,224},{224,1... | collective-permute-start | bytes 786440 | tf_op jit(solution)/shard_map/while/body/eval_jaxpr/ppermute | solution.py:16
  538.7 10.8 %collective-permute-start.4 = (bf16[1,16,16,512]{3,2,1,0:T(8,128)(2,1)S(1)}, bf16[1,16,16,512]{3,2,1,0:T(8,128)(2,1)S(1)}, u32[]{:S(2)}, u32[]{:S(2)}) collective-permute-start(bf16[1,16,16,512]{3,2,1,0:T(8,128)(2,1)S(1)} %get-tuple-element.378), channel_id=1, source_target_pairs={{0,1},{1,2},{2,3},{3,4},{4,5},{5,6},{6,7},{7,8},{8,9},{9,10},{10,1... | collective-permute-start | bytes 786440 | tf_op jit(solution)/shard_map/while/body/eval_jaxpr/ppermute | solution.py:27
  540.6 13.0 %collective-permute-start.5 = (bf16[1,16,16,512]{3,2,1,0:T(8,128)(2,1)S(1)}, bf16[1,16,16,512]{3,2,1,0:T(8,128)(2,1)S(1)}, u32[]{:S(2)}, u32[]{:S(2)}) collective-permute-start(bf16[1,16,16,512]{3,2,1,0:T(8,128)(2,1)S(1)} %get-tuple-element.378), channel_id=1, source_target_pairs={{1,0},{2,1},{3,2},{4,3},{5,4},{6,5},{7,6},{8,7},{9,8},{10,9},{11,1... | collective-permute-start | bytes 786440 | tf_op jit(solution)/shard_map/while/body/eval_jaxpr/ppermute | solution.py:29
  562.9 21.5 %collective-permute-start.1 = (bf16[1,16,16,512]{3,2,1,0:T(8,128)(2,1)S(1)}, bf16[1,16,16,512]{3,2,1,0:T(8,128)(2,1)S(1)}, u32[]{:S(2)}, u32[]{:S(2)}) collective-permute-start(bf16[1,16,16,512]{3,2,1,0:T(8,128)(2,1)S(1)} %bitcast_select_fusion.2), channel_id=1, source_target_pairs={{0,32},{32,0},{64,96},{96,64},{128,160},{160,128},{192,224},{224,1... | collective-permute-start | bytes 786440 | tf_op jit(solution)/shard_map/while/body/eval_jaxpr/ppermute | solution.py:16
  601.8 10.8 %collective-permute-start.4 = (bf16[1,16,16,512]{3,2,1,0:T(8,128)(2,1)S(1)}, bf16[1,16,16,512]{3,2,1,0:T(8,128)(2,1)S(1)}, u32[]{:S(2)}, u32[]{:S(2)}) collective-permute-start(bf16[1,16,16,512]{3,2,1,0:T(8,128)(2,1)S(1)} %get-tuple-element.378), channel_id=1, source_target_pairs={{0,1},{1,2},{2,3},{3,4},{4,5},{5,6},{6,7},{7,8},{8,9},{9,10},{10,1... | collective-permute-start | bytes 786440 | tf_op jit(solution)/shard_map/while/body/eval_jaxpr/ppermute | solution.py:27
  603.8 12.2 %collective-permute-start.5 = (bf16[1,16,16,512]{3,2,1,0:T(8,128)(2,1)S(1)}, bf16[1,16,16,512]{3,2,1,0:T(8,128)(2,1)S(1)}, u32[]{:S(2)}, u32[]{:S(2)}) collective-permute-start(bf16[1,16,16,512]{3,2,1,0:T(8,128)(2,1)S(1)} %get-tuple-element.378), channel_id=1, source_target_pairs={{1,0},{2,1},{3,2},{4,3},{5,4},{6,5},{7,6},{8,7},{9,8},{10,9},{11,1... | collective-permute-start | bytes 786440 | tf_op jit(solution)/shard_map/while/body/eval_jaxpr/ppermute | solution.py:29
  637.9 16.8 %collective-permute-start.2 = (bf16[1,16,16,512]{3,2,1,0:T(8,128)(2,1)S(1)}, bf16[1,16,16,512]{3,2,1,0:T(8,128)(2,1)S(1)}, u32[]{:S(2)}, u32[]{:S(2)}) collective-permute-start(bf16[1,16,16,512]{3,2,1,0:T(8,128)(2,1)S(1)} %collective-permute-done.1), channel_id=1, source_target_pairs={{0,64},{32,96},{64,0},{96,32},{128,192},{160,224},{192,128},{224,1... | collective-permute-start | bytes 786440 | tf_op jit(solution)/shard_map/while/body/eval_jaxpr/ppermute | solution.py:16
  664.9 10.8 %collective-permute-start.4 = (bf16[1,16,16,512]{3,2,1,0:T(8,128)(2,1)S(1)}, bf16[1,16,16,512]{3,2,1,0:T(8,128)(2,1)S(1)}, u32[]{:S(2)}, u32[]{:S(2)}) collective-permute-start(bf16[1,16,16,512]{3,2,1,0:T(8,128)(2,1)S(1)} %get-tuple-element.378), channel_id=1, source_target_pairs={{0,1},{1,2},{2,3},{3,4},{4,5},{5,6},{6,7},{7,8},{8,9},{9,10},{10,1... | collective-permute-start | bytes 786440 | tf_op jit(solution)/shard_map/while/body/eval_jaxpr/ppermute | solution.py:27
  666.8 10.7 %collective-permute-start.5 = (bf16[1,16,16,512]{3,2,1,0:T(8,128)(2,1)S(1)}, bf16[1,16,16,512]{3,2,1,0:T(8,128)(2,1)S(1)}, u32[]{:S(2)}, u32[]{:S(2)}) collective-permute-start(bf16[1,16,16,512]{3,2,1,0:T(8,128)(2,1)S(1)} %get-tuple-element.378), channel_id=1, source_target_pairs={{1,0},{2,1},{3,2},{4,3},{5,4},{6,5},{7,6},{8,7},{9,8},{10,9},{11,1... | collective-permute-start | bytes 786440 | tf_op jit(solution)/shard_map/while/body/eval_jaxpr/ppermute | solution.py:29
  679.6 10.7 %collective-permute-start = (bf16[1,16,16,512]{3,2,1,0:T(8,128)(2,1)}, bf16[1,16,16,512]{3,2,1,0:T(8,128)(2,1)S(1)}, u32[]{:S(2)}, u32[]{:S(2)}) collective-permute-start(bf16[1,16,16,512]{3,2,1,0:T(8,128)(2,1)} %get-tuple-element.343), channel_id=1, source_target_pairs={{0,32},{32,64},{64,96},{96,128},{128,160},{160,192},{192,224},{1,3... | collective-permute-start | bytes 786440 | tf_op jit(solution)/shard_map/while/body/eval_jaxpr/ppermute | solution.py:12
  699.2 17.3 %collective-permute-start.2 = (bf16[1,16,16,512]{3,2,1,0:T(8,128)(2,1)S(1)}, bf16[1,16,16,512]{3,2,1,0:T(8,128)(2,1)S(1)}, u32[]{:S(2)}, u32[]{:S(2)}) collective-permute-start(bf16[1,16,16,512]{3,2,1,0:T(8,128)(2,1)S(1)} %collective-permute-done.1), channel_id=1, source_target_pairs={{0,64},{32,96},{64,0},{96,32},{128,192},{160,224},{192,128},{224,1... | collective-permute-start | bytes 786440 | tf_op jit(solution)/shard_map/while/body/eval_jaxpr/ppermute | solution.py:16
  727.6 10.8 %collective-permute-start.4 = (bf16[1,16,16,512]{3,2,1,0:T(8,128)(2,1)S(1)}, bf16[1,16,16,512]{3,2,1,0:T(8,128)(2,1)S(1)}, u32[]{:S(2)}, u32[]{:S(2)}) collective-permute-start(bf16[1,16,16,512]{3,2,1,0:T(8,128)(2,1)S(1)} %get-tuple-element.378), channel_id=1, source_target_pairs={{0,1},{1,2},{2,3},{3,4},{4,5},{5,6},{6,7},{7,8},{8,9},{9,10},{10,1... | collective-permute-start | bytes 786440 | tf_op jit(solution)/shard_map/while/body/eval_jaxpr/ppermute | solution.py:27
  729.6 13.1 %collective-permute-start.5 = (bf16[1,16,16,512]{3,2,1,0:T(8,128)(2,1)S(1)}, bf16[1,16,16,512]{3,2,1,0:T(8,128)(2,1)S(1)}, u32[]{:S(2)}, u32[]{:S(2)}) collective-permute-start(bf16[1,16,16,512]{3,2,1,0:T(8,128)(2,1)S(1)} %get-tuple-element.378), channel_id=1, source_target_pairs={{1,0},{2,1},{3,2},{4,3},{5,4},{6,5},{7,6},{8,7},{9,8},{10,9},{11,1... | collective-permute-start | bytes 786440 | tf_op jit(solution)/shard_map/while/body/eval_jaxpr/ppermute | solution.py:29
  767.6 23.5 %collective-permute-start.3 = (bf16[1,16,16,512]{3,2,1,0:T(8,128)(2,1)S(1)}, bf16[1,16,16,512]{3,2,1,0:T(8,128)(2,1)S(1)}, u32[]{:S(2)}, u32[]{:S(2)}) collective-permute-start(bf16[1,16,16,512]{3,2,1,0:T(8,128)(2,1)S(1)} %collective-permute-done.2), channel_id=1, source_target_pairs={{0,128},{32,160},{64,192},{96,224},{128,0},{160,32},{192,64},{224,... | collective-permute-start | bytes 786440 | tf_op jit(solution)/shard_map/while/body/eval_jaxpr/ppermute | solution.py:16
  791.7 10.8 %collective-permute-start.4 = (bf16[1,16,16,512]{3,2,1,0:T(8,128)(2,1)S(1)}, bf16[1,16,16,512]{3,2,1,0:T(8,128)(2,1)S(1)}, u32[]{:S(2)}, u32[]{:S(2)}) collective-permute-start(bf16[1,16,16,512]{3,2,1,0:T(8,128)(2,1)S(1)} %get-tuple-element.378), channel_id=1, source_target_pairs={{0,1},{1,2},{2,3},{3,4},{4,5},{5,6},{6,7},{7,8},{8,9},{9,10},{10,1... | collective-permute-start | bytes 786440 | tf_op jit(solution)/shard_map/while/body/eval_jaxpr/ppermute | solution.py:27
  793.6 13.3 %collective-permute-start.5 = (bf16[1,16,16,512]{3,2,1,0:T(8,128)(2,1)S(1)}, bf16[1,16,16,512]{3,2,1,0:T(8,128)(2,1)S(1)}, u32[]{:S(2)}, u32[]{:S(2)}) collective-permute-start(bf16[1,16,16,512]{3,2,1,0:T(8,128)(2,1)S(1)} %get-tuple-element.378), channel_id=1, source_target_pairs={{1,0},{2,1},{3,2},{4,3},{5,4},{6,5},{7,6},{8,7},{9,8},{10,9},{11,1... | collective-permute-start | bytes 786440 | tf_op jit(solution)/shard_map/while/body/eval_jaxpr/ppermute | solution.py:29
  835.9 20.8 %collective-permute-start.3 = (bf16[1,16,16,512]{3,2,1,0:T(8,128)(2,1)S(1)}, bf16[1,16,16,512]{3,2,1,0:T(8,128)(2,1)S(1)}, u32[]{:S(2)}, u32[]{:S(2)}) collective-permute-start(bf16[1,16,16,512]{3,2,1,0:T(8,128)(2,1)S(1)} %collective-permute-done.2), channel_id=1, source_target_pairs={{0,128},{32,160},{64,192},{96,224},{128,0},{160,32},{192,64},{224,... | collective-permute-start | bytes 786440 | tf_op jit(solution)/shard_map/while/body/eval_jaxpr/ppermute | solution.py:16
  857.3 10.8 %collective-permute-start.4 = (bf16[1,16,16,512]{3,2,1,0:T(8,128)(2,1)S(1)}, bf16[1,16,16,512]{3,2,1,0:T(8,128)(2,1)S(1)}, u32[]{:S(2)}, u32[]{:S(2)}) collective-permute-start(bf16[1,16,16,512]{3,2,1,0:T(8,128)(2,1)S(1)} %get-tuple-element.378), channel_id=1, source_target_pairs={{0,1},{1,2},{2,3},{3,4},{4,5},{5,6},{6,7},{7,8},{8,9},{9,10},{10,1... | collective-permute-start | bytes 786440 | tf_op jit(solution)/shard_map/while/body/eval_jaxpr/ppermute | solution.py:27
  859.2 13.3 %collective-permute-start.5 = (bf16[1,16,16,512]{3,2,1,0:T(8,128)(2,1)S(1)}, bf16[1,16,16,512]{3,2,1,0:T(8,128)(2,1)S(1)}, u32[]{:S(2)}, u32[]{:S(2)}) collective-permute-start(bf16[1,16,16,512]{3,2,1,0:T(8,128)(2,1)S(1)} %get-tuple-element.378), channel_id=1, source_target_pairs={{1,0},{2,1},{3,2},{4,3},{5,4},{6,5},{7,6},{8,7},{9,8},{10,9},{11,1... | collective-permute-start | bytes 786440 | tf_op jit(solution)/shard_map/while/body/eval_jaxpr/ppermute | solution.py:29
  (50 other events, 349.6 us)
Sparse Core Ops, SparseCore 0:
  10.0 55.0 all-gather.7
  67.7 60.6 all-gather.3
  131.1 60.4 all-gather.5
  875.8 91.8 all-reduce.3
where the time goes:
time: 978 us; the launch traced here: 976 us
  waiting for transfers between devices  577 us (59%)
  starting transfers between devices  273 us (28%)
  matrix products  46.2 us (5%)
  other arithmetic  32.5 us (3%)
  loops' own time  17.3 us (2%)
  local copies, waits for them, and re-layouts  17 us (2%)
  between operations  13.2 us (1%)
    ppermute x33, waiting for transfers between devices, partner(): lax.ppermute(shard, axis, [(i, i ^ 1 << bit) for i in range(lax.axis_size...  190 us
    ppermute x33, starting transfers between devices, partner(): lax.ppermute(shard, axis, [(i, i ^ 1 << bit) for i in range(lax.axis_size...  141 us
    psum x1, waiting for transfers between devices, broadcast(): return lax.psum(jnp.where(mine, shard, jnp.zeros_like(shard)), axis)  92 us
    ppermute x11, starting transfers between devices, extended_2(): lax.ppermute(head, axis, [((i + 1) % count, i) for i in range(ends)])  73.2 us
    all_gather x1, waiting for transfers between devices, on_device(): lax.all_gather(conv_first, 'frame', axis=2, tiled=True)  63.4 us
    all_gather x1, waiting for transfers between devices, on_device(): lax.all_gather(conv_second, 'frame', axis=2, tiled=True)  63.1 us
    all_gather x1, waiting for transfers between devices, on_device(): lax.all_gather(temporal, 'frame', axis=2, tiled=True)  56.3 us
    ppermute x11, waiting for transfers between devices, passed_along(): return lax.ppermute(shard, axis, pairs)  47.2 us
  transfers between devices with their start and end apart: 70, of which 70 were waited for; matrix products, arithmetic and copies ran while one was open for 1% of the time, Pallas kernels for 0%

commit v1 on v0

--- a/solution.py
+++ b/solution.py
@@ -4,6 +4,12 @@
 from jax.sharding import PartitionSpec as P
 
 skip_scale = 0.7071067811865476
+
+
+def summed_here(x, axis):
+    blocks = lax.all_gather(x, axis, axis=0, tiled=False)
+    total = blocks.sum(axis=0)
+    return total
 
 
 def passed_along(shard, axis, by):
@@ -35,7 +41,7 @@
 
 def broadcast(shard, axis, root):
     mine = lax.axis_index(axis) == root
-    return lax.psum(jnp.where(mine, shard, jnp.zeros_like(shard)), axis)
+    return summed_here(jnp.where(mine, shard, jnp.zeros_like(shard)), axis)
 
 
 def spatial(field_in, kernel):

time: 978 us -> 1070 us (1.094)
  waiting for transfers between devices: 577 us -> 663 us
    all_gather x0 -> x1, waiting for transfers between devices: none -> 178 us  [summed_here(): blocks = lax.all_gather(x, axis, axis=0, tiled=False)]
    psum x1 -> x0, waiting for transfers between devices: 92 us -> none  [broadcast(): return lax.psum(jnp.where(mine, shard, jnp.zeros_like(shard)), axis)]
where the time goes in v1:
time: 1070 us
  waiting for transfers between devices  663 us (62%)
  starting transfers between devices  273 us (26%)
  matrix products  46.2 us (4%)
  other arithmetic  38.1 us (4%)
  loops' own time  17.3 us (2%)
  local copies, waits for them, and re-layouts  16.1 us (2%)
  between operations  13.2 us (1%)
    ppermute x33, waiting for transfers between devices, partner(): lax.ppermute(shard, axis, [(i, i ^ 1 << bit) for i in range(lax.axis_size...  190 us
    all_gather x1, waiting for transfers between devices, summed_here(): blocks = lax.all_gather(x, axis, axis=0, tiled=False)  178 us
    ppermute x33, starting transfers between devices, partner(): lax.ppermute(shard, axis, [(i, i ^ 1 << bit) for i in range(lax.axis_size...  141 us
    ppermute x11, starting transfers between devices, extended_2(): lax.ppermute(head, axis, [((i + 1) % count, i) for i in range(ends)])  73.2 us
    all_gather x1, waiting for transfers between devices, on_device(): lax.all_gather(conv_first, 'frame', axis=2, tiled=True)  63.4 us
    all_gather x1, waiting for transfers between devices, on_device(): lax.all_gather(conv_second, 'frame', axis=2, tiled=True)  63.1 us
    all_gather x1, waiting for transfers between devices, on_device(): lax.all_gather(temporal, 'frame', axis=2, tiled=True)  56.3 us
    ppermute x11, waiting for transfers between devices, passed_along(): return lax.ppermute(shard, axis, pairs)  47.2 us
  transfers between devices with their start and end apart: 70, of which 70 were waited for; matrix products, arithmetic and copies ran while one was open for 1% of the time, Pallas kernels for 0%

profile of v1, /device:TPU:2, one launch (start us, length us, event | category | flops | bytes accessed | tf_op | source)
XLA Modules:
  0.0 1066.2 jit_solution(9618768710059821589)
XLA Ops:
  8.8 56.3 %all-gather.10.cloned.1.call-done = bf16[1,3,512,512]{3,2,1,0:T(8,128)(2,1)} async-done(((bf16[1,3,16,512]{3,2,1,0:T(8,128)(2,1)}), bf16[1,3,512,512]{3,2,1,0:T(8,128)(2,1)}) %all-gather.10.cloned.1.call-update) | async-done | bytes 1572880 | tf_op jit(solution)/shard_map/all_gather | solution.py:81
  65.1 63.4 %all-gather.6.cloned.1.call-done = bf16[1,9,512,512]{3,2,1,0:T(8,128)(2,1)} async-done(((bf16[1,9,16,512]{3,2,1,0:T(8,128)(2,1)}), bf16[1,9,512,512]{3,2,1,0:T(8,128)(2,1)}) %all-gather.6.cloned.1.call-update) | async-done | bytes 4718608 | tf_op jit(solution)/shard_map/all_gather | solution.py:79
  128.4 63.1 %all-gather.8.cloned.1.call-done = bf16[1,9,512,512]{3,2,1,0:T(8,128)(2,1)} async-done(((bf16[1,9,16,512]{3,2,1,0:T(8,128)(2,1)}), bf16[1,9,512,512]{3,2,1,0:T(8,128)(2,1)}) %all-gather.8.cloned.1.call-update) | async-done | bytes 4718608 | tf_op jit(solution)/shard_map/all_gather | solution.py:80
  192.3 682.3 %while.16 = (s32[]{:T(128)}, bf16[1,16,16,512]{3,2,1,0:T(8,128)(2,1)}, bf16[4,1,16,16,512]{4,3,2,1,0:T(8,128)(2,1)S(1)}, bf16[4,1,16,16,512]{4,3,2,1,0:T(8,128)(...) while((s32[]{:T(128)}, ...), condition=%wide.region_5.6_spmd.clone, body=%wide.region_0.5_spmd.clone.sunk | while | flops 2825650176 | bytes 99615424 | solution.py:134
  234.9 6.7 collective-permute-start.5
  245.5 7.0 conditional.7
  270.5 7.6 collective-permute-done.2
  278.8 7.2 collective-permute-done.3
  293.9 6.7 collective-permute-start.5
  307.3 7.0 conditional.7
  342.1 7.3 collective-permute-done.3
  357.3 6.7 collective-permute-start.5
  370.6 7.0 conditional.7
  397.8 7.7 collective-permute-done.2
  406.1 7.2 collective-permute-done.3
  421.2 6.7 collective-permute-start.5
  434.5 7.0 conditional.7
  468.4 7.5 collective-permute-done.3
  478.5 6.7 collective-permute-start.5
  491.1 14.6 %collective-permute-start = (bf16[1,16,16,512]{3,2,1,0:T(8,128)(2,1)}, bf16[1,16,16,512]{3,2,1,0:T(8,128)(2,1)S(1)}, u32[]{:S(2)}, u32[]{:S(2)}) collective-permute-start(bf16[1,16,16,512]{3,2,1,0:T(8,128)(2,1)} %get-tuple-element.343), channel_id=1, source_target_pairs={{0,32},{32,64},{64,96},{96,128},{128,160},{160,192},{192,224},{1,3... | collective-permute-start | bytes 786440 | tf_op jit(solution)/shard_map/while/body/eval_jaxpr/ppermute | solution.py:18
  510.8 6.9 collective-permute-start.1
  531.0 7.2 collective-permute-done.3
  562.9 15.2 %collective-permute-start.1 = (bf16[1,16,16,512]{3,2,1,0:T(8,128)(2,1)S(1)}, bf16[1,16,16,512]{3,2,1,0:T(8,128)(2,1)S(1)}, u32[]{:S(2)}, u32[]{:S(2)}) collective-permute-start(bf16[1,16,16,512]{3,2,1,0:T(8,128)(2,1)S(1)} %bitcast_select_fusion.2), channel_id=1, source_target_pairs={{0,32},{32,0},{64,96},{96,64},{128,160},{160,128},{192,224},{224,1... | collective-permute-start | bytes 786440 | tf_op jit(solution)/shard_map/while/body/eval_jaxpr/ppermute | solution.py:22
  594.0 7.3 collective-permute-done.3
  603.8 6.7 collective-permute-start.5
  637.9 11.0 %collective-permute-start.2 = (bf16[1,16,16,512]{3,2,1,0:T(8,128)(2,1)S(1)}, bf16[1,16,16,512]{3,2,1,0:T(8,128)(2,1)S(1)}, u32[]{:S(2)}, u32[]{:S(2)}) collective-permute-start(bf16[1,16,16,512]{3,2,1,0:T(8,128)(2,1)S(1)} %collective-permute-done.1), channel_id=1, source_target_pairs={{0,64},{32,96},{64,0},{96,32},{128,192},{160,224},{192,128},{224,1... | collective-permute-start | bytes 786440 | tf_op jit(solution)/shard_map/while/body/eval_jaxpr/ppermute | solution.py:22
  666.8 6.7 collective-permute-start.5
  699.2 13.0 %collective-permute-start.2 = (bf16[1,16,16,512]{3,2,1,0:T(8,128)(2,1)S(1)}, bf16[1,16,16,512]{3,2,1,0:T(8,128)(2,1)S(1)}, u32[]{:S(2)}, u32[]{:S(2)}) collective-permute-start(bf16[1,16,16,512]{3,2,1,0:T(8,128)(2,1)S(1)} %collective-permute-done.1), channel_id=1, source_target_pairs={{0,64},{32,96},{64,0},{96,32},{128,192},{160,224},{192,128},{224,1... | collective-permute-start | bytes 786440 | tf_op jit(solution)/shard_map/while/body/eval_jaxpr/ppermute | solution.py:22
  767.6 19.2 %collective-permute-start.3 = (bf16[1,16,16,512]{3,2,1,0:T(8,128)(2,1)S(1)}, bf16[1,16,16,512]{3,2,1,0:T(8,128)(2,1)S(1)}, u32[]{:S(2)}, u32[]{:S(2)}) collective-permute-start(bf16[1,16,16,512]{3,2,1,0:T(8,128)(2,1)S(1)} %collective-permute-done.2), channel_id=1, source_target_pairs={{0,128},{32,160},{64,192},{96,224},{128,0},{160,32},{192,64},{224,... | collective-permute-start | bytes 786440 | tf_op jit(solution)/shard_map/while/body/eval_jaxpr/ppermute | solution.py:22
  793.6 6.7 collective-permute-start.5
  835.9 15.5 %collective-permute-start.3 = (bf16[1,16,16,512]{3,2,1,0:T(8,128)(2,1)S(1)}, bf16[1,16,16,512]{3,2,1,0:T(8,128)(2,1)S(1)}, u32[]{:S(2)}, u32[]{:S(2)}) collective-permute-start(bf16[1,16,16,512]{3,2,1,0:T(8,128)(2,1)S(1)} %collective-permute-done.2), channel_id=1, source_target_pairs={{0,128},{32,160},{64,192},{96,224},{128,0},{160,32},{192,64},{224,... | collective-permute-start | bytes 786440 | tf_op jit(solution)/shard_map/while/body/eval_jaxpr/ppermute | solution.py:22
  875.8 177.7 %all-gather.12.cloned.1.call-done = bf16[32,1,16,16,512]{4,3,2,1,0:T(8,128)(2,1)} async-done(((bf16[4,1,16,16,512]{4,3,2,1,0:T(8,128)(2,1)}), bf16[32,1,16,16,512]{4,3,2,1,0:T(8,128)(2,1)}) %all-gather.12.cloned.1.call-update) | async-done | bytes 8388624 | tf_op jit(solution)/shard_map/all_gather | solution.py:10
  (353 shorter events, 494.9 us)
Async XLA Ops:
  6.5 58.5 %all-gather.10.cloned.1.call-start = ((), (), s32[]{:S(2)}) async-start(), calls=%async_computation.2 | async-start | bytes 1622016 | tf_op jit(solution)/shard_map/all_gather | solution.py:81
  7.3 121.2 %all-gather.6.cloned.1.call-start = ((), (), s32[]{:S(2)}) async-start(), calls=%async_computation | async-start | bytes 4866048 | tf_op jit(solution)/shard_map/all_gather | solution.py:79
  8.0 183.6 %all-gather.8.cloned.1.call-start = ((), (), s32[]{:S(2)}) async-start(), calls=%async_computation.1 | async-start | bytes 4866048 | tf_op jit(solution)/shard_map/all_gather | solution.py:80
  8.7 1044.8 %all-gather.12.cloned.1.call-start = ((), (), s32[]{:S(2)}) async-start(), calls=%async_computation.3 | async-start | bytes 9437184 | tf_op jit(solution)/shard_map/all_gather | solution.py:10
  233.0 10.7 %collective-permute-start.4 = (bf16[1,16,16,512]{3,2,1,0:T(8,128)(2,1)S(1)}, bf16[1,16,16,512]{3,2,1,0:T(8,128)(2,1)S(1)}, u32[]{:S(2)}, u32[]{:S(2)}) collective-permute-start(bf16[1,16,16,512]{3,2,1,0:T(8,128)(2,1)S(1)} %get-tuple-element.378), channel_id=1, source_target_pairs={{0,1},{1,2},{2,3},{3,4},{4,5},{5,6},{6,7},{7,8},{8,9},{9,10},{10,1... | collective-permute-start | bytes 786440 | tf_op jit(solution)/shard_map/while/body/eval_jaxpr/ppermute | solution.py:33
  292.0 10.9 %collective-permute-start.4 = (bf16[1,16,16,512]{3,2,1,0:T(8,128)(2,1)S(1)}, bf16[1,16,16,512]{3,2,1,0:T(8,128)(2,1)S(1)}, u32[]{:S(2)}, u32[]{:S(2)}) collective-permute-start(bf16[1,16,16,512]{3,2,1,0:T(8,128)(2,1)S(1)} %get-tuple-element.378), channel_id=1, source_target_pairs={{0,1},{1,2},{2,3},{3,4},{4,5},{5,6},{6,7},{7,8},{8,9},{9,10},{10,1... | collective-permute-start | bytes 786440 | tf_op jit(solution)/shard_map/while/body/eval_jaxpr/ppermute | solution.py:33
  293.9 13.4 %collective-permute-start.5 = (bf16[1,16,16,512]{3,2,1,0:T(8,128)(2,1)S(1)}, bf16[1,16,16,512]{3,2,1,0:T(8,128)(2,1)S(1)}, u32[]{:S(2)}, u32[]{:S(2)}) collective-permute-start(bf16[1,16,16,512]{3,2,1,0:T(8,128)(2,1)S(1)} %get-tuple-element.378), channel_id=1, source_target_pairs={{1,0},{2,1},{3,2},{4,3},{5,4},{6,5},{7,6},{8,7},{9,8},{10,9},{11,1... | collective-permute-start | bytes 786440 | tf_op jit(solution)/shard_map/while/body/eval_jaxpr/ppermute | solution.py:35
  355.3 10.8 %collective-permute-start.4 = (bf16[1,16,16,512]{3,2,1,0:T(8,128)(2,1)S(1)}, bf16[1,16,16,512]{3,2,1,0:T(8,128)(2,1)S(1)}, u32[]{:S(2)}, u32[]{:S(2)}) collective-permute-start(bf16[1,16,16,512]{3,2,1,0:T(8,128)(2,1)S(1)} %get-tuple-element.378), channel_id=1, source_target_pairs={{0,1},{1,2},{2,3},{3,4},{4,5},{5,6},{6,7},{7,8},{8,9},{9,10},{10,1... | collective-permute-start | bytes 786440 | tf_op jit(solution)/shard_map/while/body/eval_jaxpr/ppermute | solution.py:33
  357.3 13.4 %collective-permute-start.5 = (bf16[1,16,16,512]{3,2,1,0:T(8,128)(2,1)S(1)}, bf16[1,16,16,512]{3,2,1,0:T(8,128)(2,1)S(1)}, u32[]{:S(2)}, u32[]{:S(2)}) collective-permute-start(bf16[1,16,16,512]{3,2,1,0:T(8,128)(2,1)S(1)} %get-tuple-element.378), channel_id=1, source_target_pairs={{1,0},{2,1},{3,2},{4,3},{5,4},{6,5},{7,6},{8,7},{9,8},{10,9},{11,1... | collective-permute-start | bytes 786440 | tf_op jit(solution)/shard_map/while/body/eval_jaxpr/ppermute | solution.py:35
  419.2 10.8 %collective-permute-start.4 = (bf16[1,16,16,512]{3,2,1,0:T(8,128)(2,1)S(1)}, bf16[1,16,16,512]{3,2,1,0:T(8,128)(2,1)S(1)}, u32[]{:S(2)}, u32[]{:S(2)}) collective-permute-start(bf16[1,16,16,512]{3,2,1,0:T(8,128)(2,1)S(1)} %get-tuple-element.378), channel_id=1, source_target_pairs={{0,1},{1,2},{2,3},{3,4},{4,5},{5,6},{6,7},{7,8},{8,9},{9,10},{10,1... | collective-permute-start | bytes 786440 | tf_op jit(solution)/shard_map/while/body/eval_jaxpr/ppermute | solution.py:33
  421.2 13.3 %collective-permute-start.5 = (bf16[1,16,16,512]{3,2,1,0:T(8,128)(2,1)S(1)}, bf16[1,16,16,512]{3,2,1,0:T(8,128)(2,1)S(1)}, u32[]{:S(2)}, u32[]{:S(2)}) collective-permute-start(bf16[1,16,16,512]{3,2,1,0:T(8,128)(2,1)S(1)} %get-tuple-element.378), channel_id=1, source_target_pairs={{1,0},{2,1},{3,2},{4,3},{5,4},{6,5},{7,6},{8,7},{9,8},{10,9},{11,1... | collective-permute-start | bytes 786440 | tf_op jit(solution)/shard_map/while/body/eval_jaxpr/ppermute | solution.py:35
  476.5 10.7 %collective-permute-start.4 = (bf16[1,16,16,512]{3,2,1,0:T(8,128)(2,1)S(1)}, bf16[1,16,16,512]{3,2,1,0:T(8,128)(2,1)S(1)}, u32[]{:S(2)}, u32[]{:S(2)}) collective-permute-start(bf16[1,16,16,512]{3,2,1,0:T(8,128)(2,1)S(1)} %get-tuple-element.378), channel_id=1, source_target_pairs={{0,1},{1,2},{2,3},{3,4},{4,5},{5,6},{6,7},{7,8},{8,9},{9,10},{10,1... | collective-permute-start | bytes 786440 | tf_op jit(solution)/shard_map/while/body/eval_jaxpr/ppermute | solution.py:33
  491.1 18.7 %collective-permute-start = (bf16[1,16,16,512]{3,2,1,0:T(8,128)(2,1)}, bf16[1,16,16,512]{3,2,1,0:T(8,128)(2,1)S(1)}, u32[]{:S(2)}, u32[]{:S(2)}) collective-permute-start(bf16[1,16,16,512]{3,2,1,0:T(8,128)(2,1)} %get-tuple-element.343), channel_id=1, source_target_pairs={{0,32},{32,64},{64,96},{96,128},{128,160},{160,192},{192,224},{1,3... | collective-permute-start | bytes 786440 | tf_op jit(solution)/shard_map/while/body/eval_jaxpr/ppermute | solution.py:18
  510.8 11.3 %collective-permute-start.1 = (bf16[1,16,16,512]{3,2,1,0:T(8,128)(2,1)S(1)}, bf16[1,16,16,512]{3,2,1,0:T(8,128)(2,1)S(1)}, u32[]{:S(2)}, u32[]{:S(2)}) collective-permute-start(bf16[1,16,16,512]{3,2,1,0:T(8,128)(2,1)S(1)} %bitcast_select_fusion.2), channel_id=1, source_target_pairs={{0,32},{32,0},{64,96},{96,64},{128,160},{160,128},{192,224},{224,1... | collective-permute-start | bytes 786440 | tf_op jit(solution)/shard_map/while/body/eval_jaxpr/ppermute | solution.py:22
  538.7 10.8 %collective-permute-start.4 = (bf16[1,16,16,512]{3,2,1,0:T(8,128)(2,1)S(1)}, bf16[1,16,16,512]{3,2,1,0:T(8,128)(2,1)S(1)}, u32[]{:S(2)}, u32[]{:S(2)}) collective-permute-start(bf16[1,16,16,512]{3,2,1,0:T(8,128)(2,1)S(1)} %get-tuple-element.378), channel_id=1, source_target_pairs={{0,1},{1,2},{2,3},{3,4},{4,5},{5,6},{6,7},{7,8},{8,9},{9,10},{10,1... | collective-permute-start | bytes 786440 | tf_op jit(solution)/shard_map/while/body/eval_jaxpr/ppermute | solution.py:33
  540.6 13.0 %collective-permute-start.5 = (bf16[1,16,16,512]{3,2,1,0:T(8,128)(2,1)S(1)}, bf16[1,16,16,512]{3,2,1,0:T(8,128)(2,1)S(1)}, u32[]{:S(2)}, u32[]{:S(2)}) collective-permute-start(bf16[1,16,16,512]{3,2,1,0:T(8,128)(2,1)S(1)} %get-tuple-element.378), channel_id=1, source_target_pairs={{1,0},{2,1},{3,2},{4,3},{5,4},{6,5},{7,6},{8,7},{9,8},{10,9},{11,1... | collective-permute-start | bytes 786440 | tf_op jit(solution)/shard_map/while/body/eval_jaxpr/ppermute | solution.py:35
  562.9 21.5 %collective-permute-start.1 = (bf16[1,16,16,512]{3,2,1,0:T(8,128)(2,1)S(1)}, bf16[1,16,16,512]{3,2,1,0:T(8,128)(2,1)S(1)}, u32[]{:S(2)}, u32[]{:S(2)}) collective-permute-start(bf16[1,16,16,512]{3,2,1,0:T(8,128)(2,1)S(1)} %bitcast_select_fusion.2), channel_id=1, source_target_pairs={{0,32},{32,0},{64,96},{96,64},{128,160},{160,128},{192,224},{224,1... | collective-permute-start | bytes 786440 | tf_op jit(solution)/shard_map/while/body/eval_jaxpr/ppermute | solution.py:22
  601.8 10.8 %collective-permute-start.4 = (bf16[1,16,16,512]{3,2,1,0:T(8,128)(2,1)S(1)}, bf16[1,16,16,512]{3,2,1,0:T(8,128)(2,1)S(1)}, u32[]{:S(2)}, u32[]{:S(2)}) collective-permute-start(bf16[1,16,16,512]{3,2,1,0:T(8,128)(2,1)S(1)} %get-tuple-element.378), channel_id=1, source_target_pairs={{0,1},{1,2},{2,3},{3,4},{4,5},{5,6},{6,7},{7,8},{8,9},{9,10},{10,1... | collective-permute-start | bytes 786440 | tf_op jit(solution)/shard_map/while/body/eval_jaxpr/ppermute | solution.py:33
  603.8 12.2 %collective-permute-start.5 = (bf16[1,16,16,512]{3,2,1,0:T(8,128)(2,1)S(1)}, bf16[1,16,16,512]{3,2,1,0:T(8,128)(2,1)S(1)}, u32[]{:S(2)}, u32[]{:S(2)}) collective-permute-start(bf16[1,16,16,512]{3,2,1,0:T(8,128)(2,1)S(1)} %get-tuple-element.378), channel_id=1, source_target_pairs={{1,0},{2,1},{3,2},{4,3},{5,4},{6,5},{7,6},{8,7},{9,8},{10,9},{11,1... | collective-permute-start | bytes 786440 | tf_op jit(solution)/shard_map/while/body/eval_jaxpr/ppermute | solution.py:35
  637.9 16.8 %collective-permute-start.2 = (bf16[1,16,16,512]{3,2,1,0:T(8,128)(2,1)S(1)}, bf16[1,16,16,512]{3,2,1,0:T(8,128)(2,1)S(1)}, u32[]{:S(2)}, u32[]{:S(2)}) collective-permute-start(bf16[1,16,16,512]{3,2,1,0:T(8,128)(2,1)S(1)} %collective-permute-done.1), channel_id=1, source_target_pairs={{0,64},{32,96},{64,0},{96,32},{128,192},{160,224},{192,128},{224,1... | collective-permute-start | bytes 786440 | tf_op jit(solution)/shard_map/while/body/eval_jaxpr/ppermute | solution.py:22
  664.9 10.8 %collective-permute-start.4 = (bf16[1,16,16,512]{3,2,1,0:T(8,128)(2,1)S(1)}, bf16[1,16,16,512]{3,2,1,0:T(8,128)(2,1)S(1)}, u32[]{:S(2)}, u32[]{:S(2)}) collective-permute-start(bf16[1,16,16,512]{3,2,1,0:T(8,128)(2,1)S(1)} %get-tuple-element.378), channel_id=1, source_target_pairs={{0,1},{1,2},{2,3},{3,4},{4,5},{5,6},{6,7},{7,8},{8,9},{9,10},{10,1... | collective-permute-start | bytes 786440 | tf_op jit(solution)/shard_map/while/body/eval_jaxpr/ppermute | solution.py:33
  666.8 10.7 %collective-permute-start.5 = (bf16[1,16,16,512]{3,2,1,0:T(8,128)(2,1)S(1)}, bf16[1,16,16,512]{3,2,1,0:T(8,128)(2,1)S(1)}, u32[]{:S(2)}, u32[]{:S(2)}) collective-permute-start(bf16[1,16,16,512]{3,2,1,0:T(8,128)(2,1)S(1)} %get-tuple-element.378), channel_id=1, source_target_pairs={{1,0},{2,1},{3,2},{4,3},{5,4},{6,5},{7,6},{8,7},{9,8},{10,9},{11,1... | collective-permute-start | bytes 786440 | tf_op jit(solution)/shard_map/while/body/eval_jaxpr/ppermute | solution.py:35
  679.6 10.7 collective-permute-start
  699.2 17.3 %collective-permute-start.2 = (bf16[1,16,16,512]{3,2,1,0:T(8,128)(2,1)S(1)}, bf16[1,16,16,512]{3,2,1,0:T(8,128)(2,1)S(1)}, u32[]{:S(2)}, u32[]{:S(2)}) collective-permute-start(bf16[1,16,16,512]{3,2,1,0:T(8,128)(2,1)S(1)} %collective-permute-done.1), channel_id=1, source_target_pairs={{0,64},{32,96},{64,0},{96,32},{128,192},{160,224},{192,128},{224,1... | collective-permute-start | bytes 786440 | tf_op jit(solution)/shard_map/while/body/eval_jaxpr/ppermute | solution.py:22
  727.6 10.8 %collective-permute-start.4 = (bf16[1,16,16,512]{3,2,1,0:T(8,128)(2,1)S(1)}, bf16[1,16,16,512]{3,2,1,0:T(8,128)(2,1)S(1)}, u32[]{:S(2)}, u32[]{:S(2)}) collective-permute-start(bf16[1,16,16,512]{3,2,1,0:T(8,128)(2,1)S(1)} %get-tuple-element.378), channel_id=1, source_target_pairs={{0,1},{1,2},{2,3},{3,4},{4,5},{5,6},{6,7},{7,8},{8,9},{9,10},{10,1... | collective-permute-start | bytes 786440 | tf_op jit(solution)/shard_map/while/body/eval_jaxpr/ppermute | solution.py:33
  729.6 13.1 %collective-permute-start.5 = (bf16[1,16,16,512]{3,2,1,0:T(8,128)(2,1)S(1)}, bf16[1,16,16,512]{3,2,1,0:T(8,128)(2,1)S(1)}, u32[]{:S(2)}, u32[]{:S(2)}) collective-permute-start(bf16[1,16,16,512]{3,2,1,0:T(8,128)(2,1)S(1)} %get-tuple-element.378), channel_id=1, source_target_pairs={{1,0},{2,1},{3,2},{4,3},{5,4},{6,5},{7,6},{8,7},{9,8},{10,9},{11,1... | collective-permute-start | bytes 786440 | tf_op jit(solution)/shard_map/while/body/eval_jaxpr/ppermute | solution.py:35
  767.6 23.5 %collective-permute-start.3 = (bf16[1,16,16,512]{3,2,1,0:T(8,128)(2,1)S(1)}, bf16[1,16,16,512]{3,2,1,0:T(8,128)(2,1)S(1)}, u32[]{:S(2)}, u32[]{:S(2)}) collective-permute-start(bf16[1,16,16,512]{3,2,1,0:T(8,128)(2,1)S(1)} %collective-permute-done.2), channel_id=1, source_target_pairs={{0,128},{32,160},{64,192},{96,224},{128,0},{160,32},{192,64},{224,... | collective-permute-start | bytes 786440 | tf_op jit(solution)/shard_map/while/body/eval_jaxpr/ppermute | solution.py:22
  791.7 10.8 %collective-permute-start.4 = (bf16[1,16,16,512]{3,2,1,0:T(8,128)(2,1)S(1)}, bf16[1,16,16,512]{3,2,1,0:T(8,128)(2,1)S(1)}, u32[]{:S(2)}, u32[]{:S(2)}) collective-permute-start(bf16[1,16,16,512]{3,2,1,0:T(8,128)(2,1)S(1)} %get-tuple-element.378), channel_id=1, source_target_pairs={{0,1},{1,2},{2,3},{3,4},{4,5},{5,6},{6,7},{7,8},{8,9},{9,10},{10,1... | collective-permute-start | bytes 786440 | tf_op jit(solution)/shard_map/while/body/eval_jaxpr/ppermute | solution.py:33
  793.6 13.3 %collective-permute-start.5 = (bf16[1,16,16,512]{3,2,1,0:T(8,128)(2,1)S(1)}, bf16[1,16,16,512]{3,2,1,0:T(8,128)(2,1)S(1)}, u32[]{:S(2)}, u32[]{:S(2)}) collective-permute-start(bf16[1,16,16,512]{3,2,1,0:T(8,128)(2,1)S(1)} %get-tuple-element.378), channel_id=1, source_target_pairs={{1,0},{2,1},{3,2},{4,3},{5,4},{6,5},{7,6},{8,7},{9,8},{10,9},{11,1... | collective-permute-start | bytes 786440 | tf_op jit(solution)/shard_map/while/body/eval_jaxpr/ppermute | solution.py:35
  835.9 20.8 %collective-permute-start.3 = (bf16[1,16,16,512]{3,2,1,0:T(8,128)(2,1)S(1)}, bf16[1,16,16,512]{3,2,1,0:T(8,128)(2,1)S(1)}, u32[]{:S(2)}, u32[]{:S(2)}) collective-permute-start(bf16[1,16,16,512]{3,2,1,0:T(8,128)(2,1)S(1)} %collective-permute-done.2), channel_id=1, source_target_pairs={{0,128},{32,160},{64,192},{96,224},{128,0},{160,32},{192,64},{224,... | collective-permute-start | bytes 786440 | tf_op jit(solution)/shard_map/while/body/eval_jaxpr/ppermute | solution.py:22
  857.3 10.8 %collective-permute-start.4 = (bf16[1,16,16,512]{3,2,1,0:T(8,128)(2,1)S(1)}, bf16[1,16,16,512]{3,2,1,0:T(8,128)(2,1)S(1)}, u32[]{:S(2)}, u32[]{:S(2)}) collective-permute-start(bf16[1,16,16,512]{3,2,1,0:T(8,128)(2,1)S(1)} %get-tuple-element.378), channel_id=1, source_target_pairs={{0,1},{1,2},{2,3},{3,4},{4,5},{5,6},{6,7},{7,8},{8,9},{9,10},{10,1... | collective-permute-start | bytes 786440 | tf_op jit(solution)/shard_map/while/body/eval_jaxpr/ppermute | solution.py:33
  859.2 13.3 %collective-permute-start.5 = (bf16[1,16,16,512]{3,2,1,0:T(8,128)(2,1)S(1)}, bf16[1,16,16,512]{3,2,1,0:T(8,128)(2,1)S(1)}, u32[]{:S(2)}, u32[]{:S(2)}) collective-permute-start(bf16[1,16,16,512]{3,2,1,0:T(8,128)(2,1)S(1)} %get-tuple-element.378), channel_id=1, source_target_pairs={{1,0},{2,1},{3,2},{4,3},{5,4},{6,5},{7,6},{8,7},{9,8},{10,9},{11,1... | collective-permute-start | bytes 786440 | tf_op jit(solution)/shard_map/while/body/eval_jaxpr/ppermute | solution.py:35
  (50 other events, 349.6 us)
Sparse Core Ops, SparseCore 0:
  10.0 55.0 all-gather.9
  67.7 60.6 all-gather.5
  131.1 60.4 all-gather.7
  875.9 177.5 all-gather.11
